TPU v7x, 32 devices: a whole 2x2x4 slice. The times are simulated.
32 devices in a mesh: area: 8 (over z, x), row: 4 (over y, core).
Axes of the slice: x: 2, y: 2, z: 4, core: 2. Of those that a mesh axis runs over, the one named last changes fastest.
Arguments:
- conductance_inverse: float32 [32, 1024, 1024], P(('area', 'row')), as said below
- cap_history: float32 [32, 1024, 128], P(('area', 'row')), may hold values from -3 to 3
- cap_conductance: float32 [32, 1024], P(('area', 'row')), may hold values from 0.5 to 0.8
- wave_history: float32 [32, 40, 32, 128], P(('area', 'row')), may hold values from -6 to 6
- line_partner: int32 [32, 32], P(('area', 'row')), may hold values from 0 to 31, as said below
- line_node: int32 [32, 32], P(('area', 'row')), may hold values from 0 to 1023
- line_delay: int32 [32, 32], P(('area', 'row')), may hold values from 20 to 40
- line_admittance: float32 [32, 32], P(('area', 'row')), may hold values from 0.2 to 1
- conv_node: int32 [32, 64], P(('area', 'row')), may hold values from 0 to 1023
- conv_count: int32 [32], P(('area', 'row')), may hold values from 1 to 64, as said below
- conv_state: float32 [32, 2, 64, 128], P(('area', 'row')), may hold values from -3 to 3
- conv_reference: float32 [32, 2, 64, 128], P(('area', 'row')), may hold values from -4 to 4
- conv_rate: float32 [32, 64], P(('area', 'row')), may hold values from 0.03 to 0.6
- conv_limit: float32 [32, 64], P(('area', 'row')), may hold values from 1 to 2.5
- port_node: int32 [32, 8], P(('area', 'row')), may hold values from 0 to 1023
- port_admittance: float32 [32, 8], P(('area', 'row')), may hold values from 0.3 to 1.2
- port_voltage_prev: float32 [2, 32, 8, 128], P(None, ('area', 'row')), may hold values from -5 to 5
- port_bus: int32 [32, 8], P('area'), may hold values from 0 to 20479
- transfer_impedance: float32 [2, 20480, 256], P(None, 'row', 'area'), may hold values from -0.75 to 0.75
Outputs:
- waves: float32 [32, 20, 32, 128], P(('area', 'row'))
- cap_history_out: float32 [32, 1024, 128], P(('area', 'row'))
- conv_state_out: float32 [32, 2, 64, 128], P(('area', 'row'))
- bus_voltage: float32 [2, 20480, 128], P(None, 'row')
- port_voltage: float32 [2, 32, 8, 128], P(None, ('area', 'row'))
Inputs may be any that keep to these rules, and one draw needn't show every extreme that they name: Slot l < 16 of subnetwork s and slot l + 16 of subnetwork (s + k_l) mod 32 are the two ends of one line, with k_l in 1 or 2 the same for every subnetwork and exactly 12 of the k_l equal to 1; so line_partner[s, l] = (s + k_l) mod 32 and line_partner[s, l + 16] = (s - k_l) mod 32. `conv_count`: some subnetwork has all 64 converters in service. `conductance_inverse`: each subnetwork's inverse nodal conductance matrix.
All inputs are finite; a program needn't handle non-finite values.
Results may differ from a plain program's by a relative error of at most 0.0003.
Values sent between devices are 32-bit elements; how exact they have to be, the bound alone decides.
A program may use at most 64 MiB of HBM per device.

v0:
```python
import math
import jax
import jax.numpy as jnp
from jax import lax
from jax.sharding import PartitionSpec as P

STEPS = 20
HIST = 40
NEAR = 12
HIGHEST = lax.Precision.HIGHEST
SAG_FACTOR = 0.3


def from_behind(x, axis, by):
    size = lax.axis_size(axis)
    return lax.ppermute(x, axis, [(i, (i + by) % size) for i in range(size)])


def window(
    ginv,
    start_hist,
    gcap,
    incoming,
    lnode,
    ladm,
    cnode,
    ccount,
    cstate,
    setpoint_flow,
    crate,
    climit,
    pnode,
    padm,
    pvolt,
):
    nodes = ginv.shape[0]
    lines = lnode.shape[0]
    convs = cnode.shape[0]
    index = jnp.concatenate([lnode, cnode, pnode])
    onehot = (jnp.arange(nodes, dtype=jnp.int32)[:, None] == index[None, :]).astype(jnp.float32)
    picker = onehot.T
    live = (jnp.arange(convs, dtype=jnp.int32) < ccount)[:, None]
    angles = jnp.arange(1, STEPS + 1, dtype=jnp.float32) * jnp.float32(2.0 * math.pi / STEPS)
    limit = climit[:, None]
    slew_limit = crate[:, None]

    def advance(carry, inputs):
        hist_now, inverter_axial_part, inverter_normal_part, acc_re, acc_im = carry
        inward, angle = inputs
        angle_cos_factor = jnp.cos(angle)
        angle_sin_factor = jnp.sin(angle)
        drive = jnp.where(
            live,
            inverter_axial_part * angle_cos_factor - inverter_normal_part * angle_sin_factor,
            0.0,
        )
        source = padm[:, None] * (pvolt[0] * angle_cos_factor - pvolt[1] * angle_sin_factor)
        stacked = jnp.concatenate([inward, drive, source], axis=0)
        right = hist_now + jnp.dot(onehot, stacked, precision=HIGHEST)
        volt = jnp.dot(ginv, right, precision=HIGHEST)
        probe = jnp.dot(picker, volt, precision=HIGHEST)
        at_line = probe[:lines]
        inverter_emf = probe[lines : lines + convs]
        at_port = probe[lines + convs :]
        outward = 2.0 * ladm[:, None] * at_line - inward
        flow = source - padm[:, None] * at_port
        acc_re = acc_re + flow * angle_cos_factor
        acc_im = acc_im - flow * angle_sin_factor
        unclipped_axial_part = (
            inverter_axial_part
            + slew_limit * (setpoint_flow[0] - inverter_axial_part)
            - SAG_FACTOR * inverter_emf * angle_cos_factor
        )
        unclipped_normal_part = (
            inverter_normal_part
            + slew_limit * (setpoint_flow[1] - inverter_normal_part)
            + SAG_FACTOR * inverter_emf * angle_sin_factor
        )
        inverter_axial_part = jnp.where(
            live, limit * jnp.tanh(unclipped_axial_part / limit), inverter_axial_part
        )
        inverter_normal_part = jnp.where(
            live, limit * jnp.tanh(unclipped_normal_part / limit), inverter_normal_part
        )
        hist_now = 2.0 * gcap[:, None] * volt - hist_now
        return ((hist_now, inverter_axial_part, inverter_normal_part, acc_re, acc_im), outward)

    zeros = jnp.zeros(pvolt.shape[1:], dtype=jnp.float32)
    carry = (start_hist, cstate[0], cstate[1], zeros, zeros)
    carry, outward = lax.scan(advance, carry, (incoming, angles))
    hist_end, inverter_axial_part, inverter_normal_part, acc_re, acc_im = carry
    current = jnp.stack([acc_re, acc_im]) * jnp.float32(2.0 / STEPS)
    return (outward, hist_end, jnp.stack([inverter_axial_part, inverter_normal_part]), current)


def per_device(
    conductance_inverse,
    cap_history,
    cap_conductance,
    wave_history,
    line_partner,
    line_node,
    line_delay,
    line_admittance,
    conv_node,
    conv_count,
    conv_state,
    conv_reference,
    conv_rate,
    conv_limit,
    port_node,
    port_admittance,
    port_voltage_prev,
    port_bus,
    transfer_impedance,
):
    subnets = lax.axis_size(("area", "row"))
    own = lax.axis_index(("area", "row"))
    history = wave_history[0]
    lines = history.shape[1]
    partner = line_partner[0]
    offset = (partner - own) % subnets
    signed = jnp.where(offset > subnets // 2, offset - subnets, offset)
    remote = (jnp.arange(lines, dtype=jnp.int32) + lines // 2) % lines
    combined = jnp.zeros(history.shape, jnp.float32)
    for reach in (1, -1, 2, -2):
        count = NEAR if abs(reach) == 1 else lines // 2 - NEAR
        sending = signed == reach
        order = jnp.argsort(jnp.where(sending, 0, 1), stable=True)[:count]
        packed = jnp.take(history, order, axis=1)
        arrived = from_behind(packed, ("area", "row"), reach)
        rank = jnp.cumsum(sending.astype(jnp.int32)) - 1
        slot = jnp.clip(rank[remote], 0, count - 1)
        picked = jnp.take(arrived, slot, axis=1)
        combined = combined + jnp.where((signed == -reach)[None, :, None], picked, 0.0)
    delay = line_delay[0]
    where_now = jnp.arange(STEPS, dtype=jnp.int32)[:, None] - delay[None, :] + HIST
    select = (where_now[:, None, :] == jnp.arange(HIST, dtype=jnp.int32)[None, :, None]).astype(
        jnp.float32
    )
    incoming = jnp.einsum("thl,hlc->tlc", select, combined, precision=HIGHEST)
    outward, hist_end, conv_out, current = window(
        conductance_inverse[0],
        cap_history[0],
        cap_conductance[0],
        incoming,
        line_node[0],
        line_admittance[0],
        conv_node[0],
        conv_count[0],
        conv_state[0],
        conv_reference[0],
        conv_rate[0],
        conv_limit[0],
        port_node[0],
        port_admittance[0],
        port_voltage_prev[:, 0],
    )
    bus_rows = transfer_impedance.shape[1]
    cases = current.shape[2]
    piece = lax.all_gather(current[:, None], "row", axis=1, tiled=True)
    members = piece.shape[1]
    ports = piece.shape[2]
    flat = piece.reshape(2, members * ports, cases)
    real = jnp.dot(transfer_impedance[0], flat[0], precision=HIGHEST) - jnp.dot(
        transfer_impedance[1], flat[1], precision=HIGHEST
    )
    imag = jnp.dot(transfer_impedance[0], flat[1], precision=HIGHEST) + jnp.dot(
        transfer_impedance[1], flat[0], precision=HIGHEST
    )
    partial_bus = jnp.stack([real, imag])
    bus_voltage = lax.psum(partial_bus, "area")
    first_row = lax.axis_index("row") * bus_rows
    local_bus = (port_bus - first_row).reshape(-1)
    pick_rows = (local_bus[:, None] == jnp.arange(bus_rows, dtype=jnp.int32)[None, :]).astype(
        jnp.float32
    )
    gathered = jnp.einsum("jb,xbc->xjc", pick_rows, bus_voltage, precision=HIGHEST)
    gathered = gathered.reshape(2, port_bus.shape[0], port_bus.shape[1], cases)
    port_voltage = lax.psum_scatter(gathered, "row", scatter_dimension=1, tiled=True)
    return (outward[None], hist_end[None], conv_out[None], bus_voltage, port_voltage)


def solution(mesh):
    placed = (
        P(("area", "row"), None, None),
        P(("area", "row"), None, None),
        P(("area", "row"), None),
        P(("area", "row"), None, None, None),
        P(("area", "row"), None),
        P(("area", "row"), None),
        P(("area", "row"), None),
        P(("area", "row"), None),
        P(("area", "row"), None),
        P(("area", "row")),
        P(("area", "row"), None, None, None),
        P(("area", "row"), None, None, None),
        P(("area", "row"), None),
        P(("area", "row"), None),
        P(("area", "row"), None),
        P(("area", "row"), None),
        P(None, ("area", "row"), None, None),
        P("area", None),
        P(None, "row", "area"),
    )
    return jax.shard_map(
        per_device,
        mesh=mesh,
        in_specs=placed,
        out_specs=(
            P(("area", "row"), None, None, None),
            P(("area", "row"), None, None),
            P(("area", "row"), None, None, None),
            P(None, "row", None),
            P(None, ("area", "row"), None, None),
        ),
        check_vma=False,
    )
```

profile of v0, /device:TPU:0, one launch (start us, length us, event | category | flops | bytes accessed | tf_op | source)
XLA Modules:
  0.0 522.5 jit_solution(1617881758800676381)
XLA Ops:
  7.9 1.6 sort.61
  9.6 1.5 copy.56
  11.7 3.0 collective-permute-start.2
  14.7 1.6 sort.62
  17.0 4.0 collective-permute-start.3
  20.9 1.6 sort.60
  23.3 0.9 collective-permute-start.1
  24.2 1.6 sort.59
  32.1 3.7 collective-permute-done
  36.5 1.4 gather_fusion.7
  37.9 2.7 convolution_bitcast_fusion.2
  40.6 254.0 %while.23 = (s32[]{:T(128)}, f32[1024,128]{0,1:T(8,128)S(1)}, f32[64,128]{1,0:T(8,128)S(1)}, f32[64,128]{1,0:T(8,128)S(1)}, f32[8,128]{1,0:T(8,128)S(1)}, /*inde...) while((s32[]{:T(128)}, f32[1024,128]{0,1:T(8,128)S(1)}, ...), condition=%wide.region_9.14_spmd.clone.clone.clone, body=%wide.region_8.13_spmd.clone.clone.clone.sunk | while | flops 1938803712 | bytes 8437999 | solution.py:90
  43.4 0.9 constant_dynamic-slice_fusion.3
  45.1 6.7 %bitcast_subtract_fusion.4 = (f32[1024,128]{0,1:T(8,128)S(1)}, f32[128,1024]{1,0:T(8,128)S(1)}) fusion(f32[1024,128]{0,1:T(8,128)S(1)} %get-tuple-element.591, f32[1024]{0:T(1024)S(1)} %bitcast.217, f32[1024,128]{0,1:T(8,128)S(1)} %fusion.99, f32[1024,1024]{1,0:T(8,128)} %get-tuple-element.624), kind=kOutput, calls=%fused_computation.18.clone.1 | convolution fusion | flops 1610874880 | bytes 6295552 | tf_op jit(solution)/shard_map/while/body/eval_jaxpr/dot_general | solution.py:60
  56.1 0.9 constant_dynamic-slice_fusion.3
  57.8 6.7 %bitcast_subtract_fusion.4 = (f32[1024,128]{0,1:T(8,128)S(1)}, f32[128,1024]{1,0:T(8,128)S(1)}) fusion(f32[1024,128]{0,1:T(8,128)S(1)} %get-tuple-element.591, f32[1024]{0:T(1024)S(1)} %bitcast.217, f32[1024,128]{0,1:T(8,128)S(1)} %fusion.99, f32[1024,1024]{1,0:T(8,128)} %get-tuple-element.624), kind=kOutput, calls=%fused_computation.18.clone.1 | convolution fusion | flops 1610874880 | bytes 6295552 | tf_op jit(solution)/shard_map/while/body/eval_jaxpr/dot_general | solution.py:60
  68.8 0.9 constant_dynamic-slice_fusion.3
  70.5 6.7 %bitcast_subtract_fusion.4 = (f32[1024,128]{0,1:T(8,128)S(1)}, f32[128,1024]{1,0:T(8,128)S(1)}) fusion(f32[1024,128]{0,1:T(8,128)S(1)} %get-tuple-element.591, f32[1024]{0:T(1024)S(1)} %bitcast.217, f32[1024,128]{0,1:T(8,128)S(1)} %fusion.99, f32[1024,1024]{1,0:T(8,128)} %get-tuple-element.624), kind=kOutput, calls=%fused_computation.18.clone.1 | convolution fusion | flops 1610874880 | bytes 6295552 | tf_op jit(solution)/shard_map/while/body/eval_jaxpr/dot_general | solution.py:60
  81.5 0.9 constant_dynamic-slice_fusion.3
  83.2 6.7 %bitcast_subtract_fusion.4 = (f32[1024,128]{0,1:T(8,128)S(1)}, f32[128,1024]{1,0:T(8,128)S(1)}) fusion(f32[1024,128]{0,1:T(8,128)S(1)} %get-tuple-element.591, f32[1024]{0:T(1024)S(1)} %bitcast.217, f32[1024,128]{0,1:T(8,128)S(1)} %fusion.99, f32[1024,1024]{1,0:T(8,128)} %get-tuple-element.624), kind=kOutput, calls=%fused_computation.18.clone.1 | convolution fusion | flops 1610874880 | bytes 6295552 | tf_op jit(solution)/shard_map/while/body/eval_jaxpr/dot_general | solution.py:60
  94.2 0.9 constant_dynamic-slice_fusion.3
  95.9 6.7 %bitcast_subtract_fusion.4 = (f32[1024,128]{0,1:T(8,128)S(1)}, f32[128,1024]{1,0:T(8,128)S(1)}) fusion(f32[1024,128]{0,1:T(8,128)S(1)} %get-tuple-element.591, f32[1024]{0:T(1024)S(1)} %bitcast.217, f32[1024,128]{0,1:T(8,128)S(1)} %fusion.99, f32[1024,1024]{1,0:T(8,128)} %get-tuple-element.624), kind=kOutput, calls=%fused_computation.18.clone.1 | convolution fusion | flops 1610874880 | bytes 6295552 | tf_op jit(solution)/shard_map/while/body/eval_jaxpr/dot_general | solution.py:60
  106.9 0.9 constant_dynamic-slice_fusion.3
  108.6 6.7 %bitcast_subtract_fusion.4 = (f32[1024,128]{0,1:T(8,128)S(1)}, f32[128,1024]{1,0:T(8,128)S(1)}) fusion(f32[1024,128]{0,1:T(8,128)S(1)} %get-tuple-element.591, f32[1024]{0:T(1024)S(1)} %bitcast.217, f32[1024,128]{0,1:T(8,128)S(1)} %fusion.99, f32[1024,1024]{1,0:T(8,128)} %get-tuple-element.624), kind=kOutput, calls=%fused_computation.18.clone.1 | convolution fusion | flops 1610874880 | bytes 6295552 | tf_op jit(solution)/shard_map/while/body/eval_jaxpr/dot_general | solution.py:60
  119.6 0.9 constant_dynamic-slice_fusion.3
  121.3 6.7 %bitcast_subtract_fusion.4 = (f32[1024,128]{0,1:T(8,128)S(1)}, f32[128,1024]{1,0:T(8,128)S(1)}) fusion(f32[1024,128]{0,1:T(8,128)S(1)} %get-tuple-element.591, f32[1024]{0:T(1024)S(1)} %bitcast.217, f32[1024,128]{0,1:T(8,128)S(1)} %fusion.99, f32[1024,1024]{1,0:T(8,128)} %get-tuple-element.624), kind=kOutput, calls=%fused_computation.18.clone.1 | convolution fusion | flops 1610874880 | bytes 6295552 | tf_op jit(solution)/shard_map/while/body/eval_jaxpr/dot_general | solution.py:60
  132.3 0.9 constant_dynamic-slice_fusion.3
  134.0 6.7 %bitcast_subtract_fusion.4 = (f32[1024,128]{0,1:T(8,128)S(1)}, f32[128,1024]{1,0:T(8,128)S(1)}) fusion(f32[1024,128]{0,1:T(8,128)S(1)} %get-tuple-element.591, f32[1024]{0:T(1024)S(1)} %bitcast.217, f32[1024,128]{0,1:T(8,128)S(1)} %fusion.99, f32[1024,1024]{1,0:T(8,128)} %get-tuple-element.624), kind=kOutput, calls=%fused_computation.18.clone.1 | convolution fusion | flops 1610874880 | bytes 6295552 | tf_op jit(solution)/shard_map/while/body/eval_jaxpr/dot_general | solution.py:60
  145.0 0.9 constant_dynamic-slice_fusion.3
  146.7 6.7 %bitcast_subtract_fusion.4 = (f32[1024,128]{0,1:T(8,128)S(1)}, f32[128,1024]{1,0:T(8,128)S(1)}) fusion(f32[1024,128]{0,1:T(8,128)S(1)} %get-tuple-element.591, f32[1024]{0:T(1024)S(1)} %bitcast.217, f32[1024,128]{0,1:T(8,128)S(1)} %fusion.99, f32[1024,1024]{1,0:T(8,128)} %get-tuple-element.624), kind=kOutput, calls=%fused_computation.18.clone.1 | convolution fusion | flops 1610874880 | bytes 6295552 | tf_op jit(solution)/shard_map/while/body/eval_jaxpr/dot_general | solution.py:60
  157.7 0.9 constant_dynamic-slice_fusion.3
  159.4 6.7 %bitcast_subtract_fusion.4 = (f32[1024,128]{0,1:T(8,128)S(1)}, f32[128,1024]{1,0:T(8,128)S(1)}) fusion(f32[1024,128]{0,1:T(8,128)S(1)} %get-tuple-element.591, f32[1024]{0:T(1024)S(1)} %bitcast.217, f32[1024,128]{0,1:T(8,128)S(1)} %fusion.99, f32[1024,1024]{1,0:T(8,128)} %get-tuple-element.624), kind=kOutput, calls=%fused_computation.18.clone.1 | convolution fusion | flops 1610874880 | bytes 6295552 | tf_op jit(solution)/shard_map/while/body/eval_jaxpr/dot_general | solution.py:60
  170.4 0.9 constant_dynamic-slice_fusion.3
  172.1 6.7 %bitcast_subtract_fusion.4 = (f32[1024,128]{0,1:T(8,128)S(1)}, f32[128,1024]{1,0:T(8,128)S(1)}) fusion(f32[1024,128]{0,1:T(8,128)S(1)} %get-tuple-element.591, f32[1024]{0:T(1024)S(1)} %bitcast.217, f32[1024,128]{0,1:T(8,128)S(1)} %fusion.99, f32[1024,1024]{1,0:T(8,128)} %get-tuple-element.624), kind=kOutput, calls=%fused_computation.18.clone.1 | convolution fusion | flops 1610874880 | bytes 6295552 | tf_op jit(solution)/shard_map/while/body/eval_jaxpr/dot_general | solution.py:60
  183.1 0.9 constant_dynamic-slice_fusion.3
  184.8 6.7 %bitcast_subtract_fusion.4 = (f32[1024,128]{0,1:T(8,128)S(1)}, f32[128,1024]{1,0:T(8,128)S(1)}) fusion(f32[1024,128]{0,1:T(8,128)S(1)} %get-tuple-element.591, f32[1024]{0:T(1024)S(1)} %bitcast.217, f32[1024,128]{0,1:T(8,128)S(1)} %fusion.99, f32[1024,1024]{1,0:T(8,128)} %get-tuple-element.624), kind=kOutput, calls=%fused_computation.18.clone.1 | convolution fusion | flops 1610874880 | bytes 6295552 | tf_op jit(solution)/shard_map/while/body/eval_jaxpr/dot_general | solution.py:60
  195.8 0.9 constant_dynamic-slice_fusion.3
  197.5 6.7 %bitcast_subtract_fusion.4 = (f32[1024,128]{0,1:T(8,128)S(1)}, f32[128,1024]{1,0:T(8,128)S(1)}) fusion(f32[1024,128]{0,1:T(8,128)S(1)} %get-tuple-element.591, f32[1024]{0:T(1024)S(1)} %bitcast.217, f32[1024,128]{0,1:T(8,128)S(1)} %fusion.99, f32[1024,1024]{1,0:T(8,128)} %get-tuple-element.624), kind=kOutput, calls=%fused_computation.18.clone.1 | convolution fusion | flops 1610874880 | bytes 6295552 | tf_op jit(solution)/shard_map/while/body/eval_jaxpr/dot_general | solution.py:60
  208.5 0.9 constant_dynamic-slice_fusion.3
  210.2 6.7 %bitcast_subtract_fusion.4 = (f32[1024,128]{0,1:T(8,128)S(1)}, f32[128,1024]{1,0:T(8,128)S(1)}) fusion(f32[1024,128]{0,1:T(8,128)S(1)} %get-tuple-element.591, f32[1024]{0:T(1024)S(1)} %bitcast.217, f32[1024,128]{0,1:T(8,128)S(1)} %fusion.99, f32[1024,1024]{1,0:T(8,128)} %get-tuple-element.624), kind=kOutput, calls=%fused_computation.18.clone.1 | convolution fusion | flops 1610874880 | bytes 6295552 | tf_op jit(solution)/shard_map/while/body/eval_jaxpr/dot_general | solution.py:60
  221.2 0.9 constant_dynamic-slice_fusion.3
  222.9 6.7 %bitcast_subtract_fusion.4 = (f32[1024,128]{0,1:T(8,128)S(1)}, f32[128,1024]{1,0:T(8,128)S(1)}) fusion(f32[1024,128]{0,1:T(8,128)S(1)} %get-tuple-element.591, f32[1024]{0:T(1024)S(1)} %bitcast.217, f32[1024,128]{0,1:T(8,128)S(1)} %fusion.99, f32[1024,1024]{1,0:T(8,128)} %get-tuple-element.624), kind=kOutput, calls=%fused_computation.18.clone.1 | convolution fusion | flops 1610874880 | bytes 6295552 | tf_op jit(solution)/shard_map/while/body/eval_jaxpr/dot_general | solution.py:60
  233.9 0.9 constant_dynamic-slice_fusion.3
  235.6 6.7 %bitcast_subtract_fusion.4 = (f32[1024,128]{0,1:T(8,128)S(1)}, f32[128,1024]{1,0:T(8,128)S(1)}) fusion(f32[1024,128]{0,1:T(8,128)S(1)} %get-tuple-element.591, f32[1024]{0:T(1024)S(1)} %bitcast.217, f32[1024,128]{0,1:T(8,128)S(1)} %fusion.99, f32[1024,1024]{1,0:T(8,128)} %get-tuple-element.624), kind=kOutput, calls=%fused_computation.18.clone.1 | convolution fusion | flops 1610874880 | bytes 6295552 | tf_op jit(solution)/shard_map/while/body/eval_jaxpr/dot_general | solution.py:60
  246.6 0.9 constant_dynamic-slice_fusion.3
  248.3 6.7 %bitcast_subtract_fusion.4 = (f32[1024,128]{0,1:T(8,128)S(1)}, f32[128,1024]{1,0:T(8,128)S(1)}) fusion(f32[1024,128]{0,1:T(8,128)S(1)} %get-tuple-element.591, f32[1024]{0:T(1024)S(1)} %bitcast.217, f32[1024,128]{0,1:T(8,128)S(1)} %fusion.99, f32[1024,1024]{1,0:T(8,128)} %get-tuple-element.624), kind=kOutput, calls=%fused_computation.18.clone.1 | convolution fusion | flops 1610874880 | bytes 6295552 | tf_op jit(solution)/shard_map/while/body/eval_jaxpr/dot_general | solution.py:60
  259.3 0.9 constant_dynamic-slice_fusion.3
  261.0 6.7 %bitcast_subtract_fusion.4 = (f32[1024,128]{0,1:T(8,128)S(1)}, f32[128,1024]{1,0:T(8,128)S(1)}) fusion(f32[1024,128]{0,1:T(8,128)S(1)} %get-tuple-element.591, f32[1024]{0:T(1024)S(1)} %bitcast.217, f32[1024,128]{0,1:T(8,128)S(1)} %fusion.99, f32[1024,1024]{1,0:T(8,128)} %get-tuple-element.624), kind=kOutput, calls=%fused_computation.18.clone.1 | convolution fusion | flops 1610874880 | bytes 6295552 | tf_op jit(solution)/shard_map/while/body/eval_jaxpr/dot_general | solution.py:60
  272.0 0.9 constant_dynamic-slice_fusion.3
  273.7 6.7 %bitcast_subtract_fusion.4 = (f32[1024,128]{0,1:T(8,128)S(1)}, f32[128,1024]{1,0:T(8,128)S(1)}) fusion(f32[1024,128]{0,1:T(8,128)S(1)} %get-tuple-element.591, f32[1024]{0:T(1024)S(1)} %bitcast.217, f32[1024,128]{0,1:T(8,128)S(1)} %fusion.99, f32[1024,1024]{1,0:T(8,128)} %get-tuple-element.624), kind=kOutput, calls=%fused_computation.18.clone.1 | convolution fusion | flops 1610874880 | bytes 6295552 | tf_op jit(solution)/shard_map/while/body/eval_jaxpr/dot_general | solution.py:60
  284.7 0.9 constant_dynamic-slice_fusion.3
  286.4 6.7 %bitcast_subtract_fusion.4 = (f32[1024,128]{0,1:T(8,128)S(1)}, f32[128,1024]{1,0:T(8,128)S(1)}) fusion(f32[1024,128]{0,1:T(8,128)S(1)} %get-tuple-element.591, f32[1024]{0:T(1024)S(1)} %bitcast.217, f32[1024,128]{0,1:T(8,128)S(1)} %fusion.99, f32[1024,1024]{1,0:T(8,128)} %get-tuple-element.624), kind=kOutput, calls=%fused_computation.18.clone.1 | convolution fusion | flops 1610874880 | bytes 6295552 | tf_op jit(solution)/shard_map/while/body/eval_jaxpr/dot_general | solution.py:60
  294.6 5.4 %all_gather.3 = f32[2,4,8,128]{3,2,1,0:T(8,128)S(1)} all-gather(f32[2,1,8,128]{3,2,1,0:T(8,128)S(1)} %maximum_multiply_fusion), channel_id=1, replica_groups=mesh['area'=8,'row'=4] {'row'}, dimensions={1}, use_global_device_ids=true | all-gather | bytes 40960 | tf_op jit(solution)/shard_map/all_gather | solution.py:161
  300.0 2.2 fusion.39
  302.2 2.2 fusion.41
  304.5 2.3 fusion.36
  306.8 2.3 fusion.35
  309.0 2.9 pad_maximum_fusion
  313.4 1.0 copy.48
  315.0 177.5 %all-reduce.3.cloned.1.call-done = f32[2,5120,128]{1,2,0:T(8,128)} async-done(((f32[2,5120,128]{1,2,0:T(8,128)}), f32[2,5120,128]{1,2,0:T(8,128)}) %all-reduce.3.cloned.1.call-update) | async-done | bytes 5242896 | tf_op jit(solution)/shard_map/psum | solution.py:172
  492.5 5.2 convolution_bitcast_fusion.3
  497.7 10.9 %all-reduce = f32[2,4,8,128]{3,2,1,0:T(8,128)S(1)} all-reduce(f32[2,4,8,128]{3,2,1,0:T(8,128)S(1)} %convolution_bitcast_fusion.3), channel_id=2, replica_groups=mesh['area'=8,'row'=4] {'row'}, use_global_device_ids=true, to_apply=%region_11.16.clone | all-reduce | flops 8192 | bytes 65536
  508.6 1.2 constant_dynamic-slice_fusion.1
  509.8 5.9 %copy.50 = f32[2,5120,128]{2,1,0:T(8,128)} copy(f32[2,5120,128]{1,2,0:T(8,128)} %all-reduce.3.cloned.1.call-done) | data formatting | bytes 10485760
  (322 shorter events, 82.7 us)
Async XLA Ops:
  7.2 19.4 %copy-start.11 = (s32[1,32]{1,0:T(1,128)S(1)}, s32[1,32]{1,0:T(1,128)}, u32[]{:S(2)}) copy-start(s32[1,32]{1,0:T(1,128)} %param.33) | copy-start | bytes 388
  7.2 19.6 %copy-start.10 = (s32[1,32]{1,0:T(1,128)S(1)}, s32[1,32]{1,0:T(1,128)}, u32[]{:S(2)}) copy-start(s32[1,32]{1,0:T(1,128)} %param.35) | copy-start | bytes 388
  7.2 485.3 %all-reduce.3.cloned.1.call-start = ((), (), s32[]{:S(2)}) async-start(), calls=%async_computation | async-start | bytes 10485760 | tf_op jit(solution)/shard_map/psum | solution.py:172
  11.6 18.9 %copy-start.5 = (f32[1,2,64,128]{3,2,1,0:T(8,128)S(1)}, f32[1,2,64,128]{3,2,1,0:T(8,128)}, u32[]{:S(2)}) copy-start(f32[1,2,64,128]{3,2,1,0:T(8,128)} %param.39) | copy-start | bytes 196612
  11.7 19.8 %collective-permute-start.2 = (f32[40,4,128]{2,0,1:T(8,128)S(1)}, f32[40,4,128]{2,0,1:T(8,128)S(1)}, u32[]{:S(2)}, u32[]{:S(2)}) collective-permute-start(f32[40,4,128]{2,0,1:T(8,128)S(1)} %select_bitcast_fusion.3), channel_id=1, source_target_pairs={{0,2},{1,3},{2,4},{3,5},{4,6},{5,7},{6,8},{7,9},{8,10},{9,11},{10,... | collective-permute-start | bytes 245768 | tf_op jit(solution)/shard_map/ppermute | solution.py:16
  16.3 14.3 %copy-start.3 = (f32[1,1024,128]{2,1,0:T(8,128)S(1)}, f32[1,1024,128]{2,1,0:T(8,128)}, u32[]{:S(2)}) copy-start(f32[1,1024,128]{2,1,0:T(8,128)} %param.30) | copy-start | bytes 1572868
  17.0 13.9 %collective-permute-start.3 = (f32[40,4,128]{2,0,1:T(8,128)S(1)}, f32[40,4,128]{2,0,1:T(8,128)S(1)}, u32[]{:S(2)}, u32[]{:S(2)}) collective-permute-start(f32[40,4,128]{2,0,1:T(8,128)S(1)} %select_bitcast_fusion.2), channel_id=1, source_target_pairs={{0,30},{1,31},{2,0},{3,1},{4,2},{5,3},{6,4},{7,5},{8,6},{9,7},{10,... | collective-permute-start | bytes 245768 | tf_op jit(solution)/shard_map/ppermute | solution.py:16
  23.1 7.7 %copy-start.12 = (s32[1,8]{1,0:T(1,128)S(1)}, s32[1,8]{1,0:T(1,128)}, u32[]{:S(2)}) copy-start(s32[1,8]{1,0:T(1,128)} %param.43) | copy-start | bytes 100
  23.1 7.7 %copy-start.13 = (s32[1,64]{1,0:T(1,128)S(1)}, s32[1,64]{1,0:T(1,128)}, u32[]{:S(2)}) copy-start(s32[1,64]{1,0:T(1,128)} %param.37) | copy-start | bytes 772
  23.2 7.6 %copy-start.14 = (s32[1,32]{1,0:T(1,128)S(1)}, s32[1,32]{1,0:T(1,128)}, u32[]{:S(2)}) copy-start(s32[1,32]{1,0:T(1,128)} %param.34) | copy-start | bytes 388
  23.3 13.2 %collective-permute-start.1 = (f32[40,12,128]{2,0,1:T(8,128)S(1)}, f32[40,12,128]{2,0,1:T(8,128)S(1)}, u32[]{:S(2)}, u32[]{:S(2)}) collective-permute-start(f32[40,12,128]{2,0,1:T(8,128)S(1)} %select_bitcast_fusion), channel_id=1, source_target_pairs={{0,31},{1,0},{2,1},{3,2},{4,3},{5,4},{6,5},{7,6},{8,7},{9,8},{10,9... | collective-permute-start | bytes 737288 | tf_op jit(solution)/shard_map/ppermute | solution.py:16
  26.5 9.3 %collective-permute-start = (f32[40,12,128]{2,0,1:T(8,128)S(1)}, f32[40,12,128]{2,0,1:T(8,128)S(1)}, u32[]{:S(2)}, u32[]{:S(2)}) collective-permute-start(f32[40,12,128]{2,0,1:T(8,128)S(1)} %select_bitcast_fusion.1), channel_id=1, source_target_pairs={{0,1},{1,2},{2,3},{3,4},{4,5},{5,6},{6,7},{7,8},{8,9},{9,10},{10,1... | collective-permute-start | bytes 737288 | tf_op jit(solution)/shard_map/ppermute | solution.py:16
  36.4 4.2 copy-start.1
  36.4 4.2 copy-start.2
  36.4 4.2 copy-start.4
  36.4 4.2 copy-start.6
  36.4 4.2 copy-start.7
  36.4 4.2 copy-start.8
  36.4 4.2 copy-start.15
  40.6 259.4 %copy-start = (f32[2,5120,32]{1,2,0:T(8,128)S(1)}, f32[2,5120,32]{1,2,0:T(8,128)}, u32[]{:S(2)}) copy-start(f32[2,5120,32]{1,2,0:T(8,128)} %param.47) | copy-start | bytes 3932164
  312.0 0.7 copy-start.9
  312.0 0.8 copy-start.16
Sparse Core Ops, SparseCore 0:
  312.1 180.2 all-reduce.2
where the time goes:
time: 525 us; the launch traced here: 523 us
  waiting for transfers between devices  181 us (34%)
  matrix products  178 us (34%)
  local copies, waits for them, and re-layouts  49.6 us (9%)
  other arithmetic  45.4 us (9%)
  loops' own time  29.9 us (6%)
  blocking collectives  16.3 us (3%)
  between operations  14.6 us (3%)
  starting transfers between devices  8.01 us (2%)
    psum x1, waiting for transfers between devices, per_device(): bus_voltage = lax.psum(partial_bus, 'area')  177 us
    dot_general x20, matrix products, advance(): volt = jnp.dot(ginv, right, precision=HIGHEST)  134 us
    dynamic_slice x40, local copies, waits for them, and re-layouts, window(): carry, outward = lax.scan(advance, carry, (incoming, angles))  30 us
    another operation x1, loops' own time, window(): carry, outward = lax.scan(advance, carry, (incoming, angles))  29.9 us
    dynamic_update_slice x20, other arithmetic, window(): carry, outward = lax.scan(advance, carry, (incoming, angles))  13.7 us
    dot_general x20, matrix products, advance(): probe = jnp.dot(picker, volt, precision=HIGHEST)  13.4 us
    broadcast_in_dim x20, other arithmetic, advance(): jnp.where(live, inverter_axial_part * angle_cos_factor - inverter_normal_...  13.1 us
    dot_general x20, matrix products, advance(): right = hist_now + jnp.dot(onehot, stacked, precision=HIGHEST)  12.9 us
  transfers between devices with their start and end apart: 5, of which 2 were waited for; matrix products, arithmetic and copies ran while one was open for 3% of the time, Pallas kernels for 0%

commit v1 on v0

--- a/solution.py
+++ b/solution.py
@@ -3,6 +3,7 @@
 import jax.numpy as jnp
 from jax import lax
 from jax.sharding import PartitionSpec as P
+from jax.lax import all_gather
 
 STEPS = 20
 HIST = 40
@@ -169,7 +170,12 @@
         transfer_impedance[1], flat[0], precision=HIGHEST
     )
     partial_bus = jnp.stack([real, imag])
-    bus_voltage = lax.psum(partial_bus, "area")
+
+    def _pack_trails(in_array):
+        upper = jnp.sum(all_gather(in_array, axis_name="area"), 0)
+        return upper
+
+    bus_voltage = _pack_trails(partial_bus)
     first_row = lax.axis_index("row") * bus_rows
     local_bus = (port_bus - first_row).reshape(-1)
     pick_rows = (local_bus[:, None] == jnp.arange(bus_rows, dtype=jnp.int32)[None, :]).astype(

time: 525 us -> 1160 us (2.21)
  waiting for transfers between devices: 181 us -> 792 us
  other arithmetic: 45.4 us -> 63.2 us
    all_gather x0 -> x1, waiting for transfers between devices: none -> 789 us  [_pack_trails(): upper = jnp.sum(all_gather(in_array, axis_name='area'), 0)]
    psum x1 -> x0, waiting for transfers between devices: 177 us -> none  [per_device(): bus_voltage = lax.psum(partial_bus, 'area')]
    unnamed x2 -> x3, other arithmetic: 0.01 us -> 17.1 us
  transfers between devices with their start and end apart: 5 -> 5, of which waited for: 2 -> 2; matrix products, arithmetic and copies ran while one was open for 3% -> 1% of each run, Pallas kernels for 0% -> 0%
where the time goes in v1:
time: 1160 us; the launch traced here: 1150 us
  waiting for transfers between devices  792 us (68%)
  matrix products  177 us (15%)
  other arithmetic  63.2 us (5%)
  local copies, waits for them, and re-layouts  49.7 us (4%)
  loops' own time  30 us (3%)
  blocking collectives  16.3 us (1%)
  between operations  14.5 us (1%)
    all_gather x1, waiting for transfers between devices, _pack_trails(): upper = jnp.sum(all_gather(in_array, axis_name='area'), 0)  789 us
    dot_general x20, matrix products, advance(): volt = jnp.dot(ginv, right, precision=HIGHEST)  134 us
    dynamic_slice x40, local copies, waits for them, and re-layouts, window(): carry, outward = lax.scan(advance, carry, (incoming, angles))  30 us
    another operation x1, loops' own time, window(): carry, outward = lax.scan(advance, carry, (incoming, angles))  30 us
  transfers between devices with their start and end apart: 5, of which 2 were waited for; matrix products, arithmetic and copies ran while one was open for 1% of the time, Pallas kernels for 0%

profile of v1, /device:TPU:0, one launch (start us, length us, event | category | flops | bytes accessed | tf_op | source)
XLA Modules:
  0.0 1154.4 jit_solution(5795788118191857820)
XLA Ops:
  7.2 1.5 copy.55
  9.4 1.6 sort.62
  11.7 7.0 collective-permute-start.3
  18.6 1.6 sort.61
  20.9 1.6 sort.60
  23.3 4.5 collective-permute-start.1
  27.8 1.6 sort.59
  37.0 3.2 collective-permute-done
  40.2 1.4 gather_fusion.5
  41.6 2.7 convolution_bitcast_fusion.2
  44.4 254.0 %while.23 = (s32[]{:T(128)}, f32[1024,128]{0,1:T(8,128)S(1)}, f32[64,128]{1,0:T(8,128)S(1)}, f32[64,128]{1,0:T(8,128)S(1)}, f32[8,128]{1,0:T(8,128)S(1)}, /*inde...) while((s32[]{:T(128)}, f32[1024,128]{0,1:T(8,128)S(1)}, ...), condition=%wide.region_9.14_spmd.clone.clone.clone, body=%wide.region_8.13_spmd.clone.clone.clone.sunk | while | flops 1938803712 | bytes 8437999 | solution.py:91
  47.3 0.9 constant_dynamic-slice_fusion.3
  48.8 6.7 bitcast_subtract_fusion.4
  60.0 0.9 constant_dynamic-slice_fusion.3
  61.5 6.7 bitcast_subtract_fusion.4
  72.7 0.9 constant_dynamic-slice_fusion.3
  74.2 6.7 bitcast_subtract_fusion.4
  85.4 0.9 constant_dynamic-slice_fusion.3
  86.9 6.7 bitcast_subtract_fusion.4
  98.1 0.9 constant_dynamic-slice_fusion.3
  99.6 6.7 bitcast_subtract_fusion.4
  110.8 0.9 constant_dynamic-slice_fusion.3
  112.3 6.7 bitcast_subtract_fusion.4
  123.5 0.9 constant_dynamic-slice_fusion.3
  125.0 6.7 bitcast_subtract_fusion.4
  136.2 0.9 constant_dynamic-slice_fusion.3
  137.7 6.7 bitcast_subtract_fusion.4
  148.9 0.9 constant_dynamic-slice_fusion.3
  150.4 6.7 bitcast_subtract_fusion.4
  161.6 0.9 constant_dynamic-slice_fusion.3
  163.1 6.7 bitcast_subtract_fusion.4
  174.2 0.9 constant_dynamic-slice_fusion.3
  175.8 6.7 bitcast_subtract_fusion.4
  186.9 0.9 constant_dynamic-slice_fusion.3
  188.5 6.7 bitcast_subtract_fusion.4
  199.6 0.9 constant_dynamic-slice_fusion.3
  201.2 6.7 bitcast_subtract_fusion.4
  212.3 0.9 constant_dynamic-slice_fusion.3
  213.9 6.7 bitcast_subtract_fusion.4
  225.0 0.9 constant_dynamic-slice_fusion.3
  226.6 6.7 bitcast_subtract_fusion.4
  237.7 0.9 constant_dynamic-slice_fusion.3
  239.3 6.7 bitcast_subtract_fusion.4
  250.4 0.9 constant_dynamic-slice_fusion.3
  252.0 6.7 bitcast_subtract_fusion.4
  263.1 0.9 constant_dynamic-slice_fusion.3
  264.7 6.7 bitcast_subtract_fusion.4
  275.8 0.9 constant_dynamic-slice_fusion.3
  277.4 6.7 bitcast_subtract_fusion.4
  288.5 0.9 constant_dynamic-slice_fusion.3
  290.1 6.7 bitcast_subtract_fusion.4
  298.4 5.4 all_gather.9
  303.8 2.3 fusion.39
  306.0 2.2 fusion.41
  308.3 2.3 fusion.36
  310.5 2.3 fusion.35
  312.8 2.9 pad_maximum_fusion
  315.7 6.0 copy.45
  323.1 1.0 copy.44
  324.8 789.1 %all-gather.3.cloned.1.call-done = f32[16,5120,128]{2,1,0:T(8,128)} async-done(((f32[2,5120,128]{2,1,0:T(8,128)}), f32[16,5120,128]{2,1,0:T(8,128)}) %all-gather.3.cloned.1.call-update) | async-done | bytes 41943056 | tf_op jit(solution)/shard_map/all_gather | solution.py:175
  1113.8 17.1 %reduce_sum.9 = f32[2,5120,128]{2,1,0:T(8,128)} reduce(f32[8,2,5120,128]{3,2,1,0:T(8,128)} %bitcast.207, f32[]{:T(128)} %constant.83.clone.1), dimensions={0}, to_apply=%region_10.15 | reduce | flops 9175040 | bytes 47185924
  1130.9 4.5 convolution_bitcast_fusion.3
  1135.4 10.9 all-reduce
  1146.4 1.2 constant_dynamic-slice_fusion.1
  (323 shorter events, 83.3 us)
Async XLA Ops:
  7.2 23.6 %copy-start.11 = (s32[1,32]{1,0:T(1,128)S(1)}, s32[1,32]{1,0:T(1,128)}, u32[]{:S(2)}) copy-start(s32[1,32]{1,0:T(1,128)} %param.33) | copy-start | bytes 388
  7.2 23.7 %copy-start.5 = (f32[1,2,64,128]{3,2,1,0:T(8,128)S(1)}, f32[1,2,64,128]{3,2,1,0:T(8,128)}, u32[]{:S(2)}) copy-start(f32[1,2,64,128]{3,2,1,0:T(8,128)} %param.39) | copy-start | bytes 196612
  7.2 1106.6 %all-gather.3.cloned.1.call-start = ((), (), s32[]{:S(2)}) async-start(), calls=%async_computation | async-start | bytes 47185920 | tf_op jit(solution)/shard_map/all_gather | solution.py:175
  11.7 23.4 %collective-permute-start.3 = (f32[40,4,128]{2,0,1:T(8,128)S(1)}, f32[40,4,128]{2,0,1:T(8,128)S(1)}, u32[]{:S(2)}, u32[]{:S(2)}) collective-permute-start(f32[40,4,128]{2,0,1:T(8,128)S(1)} %select_bitcast_fusion.2), channel_id=1, source_target_pairs={{0,30},{1,31},{2,0},{3,1},{4,2},{5,3},{6,4},{7,5},{8,6},{9,7},{10,... | collective-permute-start | bytes 245768 | tf_op jit(solution)/shard_map/ppermute | solution.py:17
  20.3 14.4 %copy-start.10 = (s32[1,32]{1,0:T(1,128)S(1)}, s32[1,32]{1,0:T(1,128)}, u32[]{:S(2)}) copy-start(s32[1,32]{1,0:T(1,128)} %param.35) | copy-start | bytes 388
  20.3 14.5 %copy-start.3 = (f32[1,1024,128]{2,1,0:T(8,128)S(1)}, f32[1,1024,128]{2,1,0:T(8,128)}, u32[]{:S(2)}) copy-start(f32[1,1024,128]{2,1,0:T(8,128)} %param.30) | copy-start | bytes 1572868
  20.9 14.8 %collective-permute-start.2 = (f32[40,4,128]{2,0,1:T(8,128)S(1)}, f32[40,4,128]{2,0,1:T(8,128)S(1)}, u32[]{:S(2)}, u32[]{:S(2)}) collective-permute-start(f32[40,4,128]{2,0,1:T(8,128)S(1)} %select_bitcast_fusion.3), channel_id=1, source_target_pairs={{0,2},{1,3},{2,4},{3,5},{4,6},{5,7},{6,8},{7,9},{8,10},{9,11},{10,... | collective-permute-start | bytes 245768 | tf_op jit(solution)/shard_map/ppermute | solution.py:17
  23.1 11.8 %copy-start.12 = (s32[1,8]{1,0:T(1,128)S(1)}, s32[1,8]{1,0:T(1,128)}, u32[]{:S(2)}) copy-start(s32[1,8]{1,0:T(1,128)} %param.43) | copy-start | bytes 100
  23.1 11.8 %copy-start.13 = (s32[1,64]{1,0:T(1,128)S(1)}, s32[1,64]{1,0:T(1,128)}, u32[]{:S(2)}) copy-start(s32[1,64]{1,0:T(1,128)} %param.37) | copy-start | bytes 772
  23.2 11.8 %copy-start.14 = (s32[1,32]{1,0:T(1,128)S(1)}, s32[1,32]{1,0:T(1,128)}, u32[]{:S(2)}) copy-start(s32[1,32]{1,0:T(1,128)} %param.34) | copy-start | bytes 388
  23.3 13.0 %collective-permute-start.1 = (f32[40,12,128]{2,0,1:T(8,128)S(1)}, f32[40,12,128]{2,0,1:T(8,128)S(1)}, u32[]{:S(2)}, u32[]{:S(2)}) collective-permute-start(f32[40,12,128]{2,0,1:T(8,128)S(1)} %select_bitcast_fusion), channel_id=1, source_target_pairs={{0,31},{1,0},{2,1},{3,2},{4,3},{5,4},{6,5},{7,6},{8,7},{9,8},{10,9... | collective-permute-start | bytes 737288 | tf_op jit(solution)/shard_map/ppermute | solution.py:17
  30.8 9.4 collective-permute-start
  36.9 7.4 copy-start.1
  36.9 7.4 copy-start.2
  36.9 7.4 copy-start.4
  36.9 7.4 copy-start.6
  37.0 7.4 copy-start.7
  37.0 7.4 copy-start.8
  37.0 7.4 copy-start.15
  44.4 259.4 %copy-start = (f32[2,5120,32]{1,2,0:T(8,128)S(1)}, f32[2,5120,32]{1,2,0:T(8,128)}, u32[]{:S(2)}) copy-start(f32[2,5120,32]{1,2,0:T(8,128)} %param.47) | copy-start | bytes 3932164
  321.7 0.7 copy-start.9
  321.7 0.8 copy-start.16
Sparse Core Ops, SparseCore 0:
  321.9 791.9 all-gather.2
